TPU v7x, 32 devices: a whole 2x2x4 slice. The times are simulated.
32 devices in a mesh: lvl: 4 (over y, x), gz: 4 (over z), gy: 2 (over core).
Axes of the slice: x: 2, y: 2, z: 4, core: 2. Of those that a mesh axis runs over, the one named last changes fastest.
Arguments:
- fine_field: float32 [32, 512, 1024], P('gz', 'gy', 'lvl'), may hold values from -1.2 to 1.2
- noise_pair: float32 [2, 32, 512, 1024], P(None, 'gz', 'gy', 'lvl'), may hold values from -4 to 4
Outputs:
- fine_next: float32 [32, 512, 1024], P('gz', 'gy', 'lvl')
- correction: float32 [16, 256, 512], P('gz', 'gy', 'lvl')
All inputs are finite; a program needn't handle non-finite values.
Results may differ from a plain program's by a relative error of at most 0.00014.
Values sent between devices are 32-bit elements; how exact they have to be, the bound alone decides.
A program may use at most 64 MiB of HBM per device.

v0:
```python
import jax
import jax.numpy as jnp
from jax import lax
from jax.sharding import PartitionSpec as P

noise_amp = 0.3


def padded_2(cells, sides, width):
    for axis, dim in sides:
        count = lax.axis_size(axis)
        head = lax.slice_in_dim(cells, 0, width, axis=dim)
        tail = lax.slice_in_dim(cells, cells.shape[dim] - width, cells.shape[dim], axis=dim)
        cells = jnp.concatenate(
            [
                lax.ppermute(tail, axis, [(i, (i + 1) % count) for i in range(count)]),
                cells,
                lax.ppermute(head, axis, [((i + 1) % count, i) for i in range(count)]),
            ],
            axis=dim,
        )
    return cells


def neighbours(padded):
    beside = padded[2:, 1:-1, 1:-1] + padded[:-2, 1:-1, 1:-1]
    beside = beside + padded[1:-1, 2:, 1:-1] + padded[1:-1, :-2, 1:-1]
    beside = beside + padded[1:-1, 1:-1, 2:] + padded[1:-1, 1:-1, :-2]
    return beside


def advance(padded, forcing, spread, react):
    center = padded[1:-1, 1:-1, 1:-1]
    return (
        center
        + spread * (neighbours(padded) - 6.0 * center)
        + react * (center - center * center * center)
        + noise_amp * forcing
    )


def coarsen(values):
    first, second, third = values.shape
    half = third // 2
    source = lax.broadcasted_iota(jnp.int32, (third, half), 0) // 2
    target = lax.broadcasted_iota(jnp.int32, (third, half), 1)
    table = (source == target).astype(jnp.float32)
    paired = jnp.dot(
        values.reshape(first * second, third),
        table,
        precision=lax.Precision.HIGHEST,
        preferred_element_type=jnp.float32,
    )
    paired = paired.reshape(first // 2, 2, second // 2, 2 * half)
    summed = paired[:, 0] + paired[:, 1]
    return (summed[:, :, :half] + summed[:, :, half:]) * 0.125


def fine_rim(values):
    return padded_2(values, (("lvl", 2), ("gz", 0), ("gy", 1)), 1)


def on_device(fine_field, noise_pair):
    coarse_padded = None
    middle = advance(fine_rim(fine_field), noise_pair[0], 0.15, 0.1)
    fine_next = advance(fine_rim(middle), noise_pair[1], 0.15, 0.1)
    coarse_noise = coarsen(noise_pair[0] + noise_pair[1])
    coarse_start = coarsen(fine_field)
    coarse_padded = padded_2(coarse_start, (("lvl", 2), ("gz", 0), ("gy", 1)), 1)
    coarse_next = advance(coarse_padded, coarse_noise, 0.075, 0.2)
    return (fine_next, coarsen(fine_next) - coarse_next)


def solution(mesh):
    in_specs = (P("gz", "gy", "lvl"), P(None, "gz", "gy", "lvl"))
    out_specs = (P("gz", "gy", "lvl"), P("gz", "gy", "lvl"))
    return jax.shard_map(
        on_device, mesh=mesh, in_specs=in_specs, out_specs=out_specs, check_vma=False
    )
```

profile of v0, /device:TPU:0, one launch (start us, length us, event | category | flops | bytes accessed | tf_op | source)
XLA Modules:
  0.0 97.1 jit_solution(4819630641351115425)
XLA Ops:
  0.6 2.9 %fusion.55 = (f32[8,256,1]{2,1,0:T(8,128)S(1)}, f32[8,256,1]{2,1,0:T(8,128)}) fusion(f32[8,256,256]{2,1,0:T(8,128)} %param.2), kind=kLoop, calls=%fused_computation.152 | loop fusion | bytes 32768 | tf_op jit(solution)/shard_map/slice | solution.py:12
  3.5 1.7 %copy.49 = f32[8,256,1]{1,0,2:T(8,128)S(1)} copy(f32[8,256,1]{2,1,0:T(8,128)} %get-tuple-element.15) | data formatting | bytes 16384
  5.2 3.0 %collective-permute-start = (f32[8,256,1]{1,0,2:T(8,128)S(1)}, f32[8,256,1]{1,0,2:T(8,128)S(1)}, u32[]{:S(2)}, u32[]{:S(2)}) collective-permute-start(f32[8,256,1]{1,0,2:T(8,128)S(1)} %copy.49), channel_id=1, source_target_pairs={{0,8},{8,16},{16,24},{24,0},{1,9},{9,17},{17,25},{25,1},{2,10},{10... | collective-permute-start | bytes 24584 | tf_op jit(solution)/shard_map/ppermute | solution.py:16
  8.2 0.3 copy.50
  8.5 1.0 %collective-permute-start.1 = (f32[8,256,1]{1,0,2:T(8,128)S(1)}, f32[8,256,1]{1,0,2:T(8,128)S(1)}, u32[]{:S(2)}, u32[]{:S(2)}) collective-permute-start(f32[8,256,1]{1,0,2:T(8,128)S(1)} %copy.50), channel_id=1, source_target_pairs={{8,0},{16,8},{24,16},{0,24},{9,1},{17,9},{25,17},{1,25},{10,2},{18... | collective-permute-start | bytes 24584 | tf_op jit(solution)/shard_map/ppermute | solution.py:18
  9.5 1.4 %convolution_bitcast_fusion = f32[2048,128]{0,1:T(8,128)S(1)} fusion(f32[2048,256]{1,0:T(8,128)S(1)} %bitcast.38, s32[256]{0:T(256)S(1)} %get-tuple-element.22, s32[256]{0:T(256)S(1)} %get-tuple-element.23, pred[256]{0:T(512)(128)(4,1)S(1)} %compare_and_fusion), kind=kOutput, calls=%fused_computation.2 | convolution fusion | flops 805404672 | bytes 3148032 | tf_op jit(solution)/shard_map/dot_general | solution.py:48
  10.9 1.3 %copy.46 = f32[2048,128]{1,0:T(8,128)} copy(f32[2048,128]{0,1:T(8,128)S(1)} %convolution_bitcast_fusion) | data formatting | bytes 2097152 | tf_op jit(solution)/shard_map/dot_general | solution.py:48
  12.2 1.5 %reshape.33 = f32[4,2,128,256]{3,2,1,0:T(8,128)S(1)} reshape(f32[2048,128]{1,0:T(8,128)} %copy.46) | data formatting | bytes 2097152 | tf_op jit(solution)/shard_map/reshape | solution.py:54
  13.8 0.9 fusion.24
  14.6 0.4 copy.34
  15.0 1.3 %copy.35 = f32[8,256,1]{2,1,0:T(8,128)} copy(f32[8,256,1]{1,0,2:T(8,128)S(1)} %collective-permute-done.1) | data formatting | bytes 16384 | tf_op jit(solution)/shard_map/ppermute | solution.py:18
  16.4 1.4 %pad_maximum_fusion.39 = (f32[1,256,258]{2,1,0:T(8,128)S(1)}, f32[1,256,258]{2,1,0:T(8,128)S(1)}) fusion(f32[8,256,1]{2,1,0:T(8,128)} %copy.35, f32[8,256,256]{2,1,0:T(8,128)S(1)} %copy-done, f32[8,256,1]{2,1,0:T(8,128)S(1)} %copy.34), kind=kLoop, calls=%fused_computation.75 | loop fusion | flops 264192 | bytes 2641920 | tf_op jit(solution)/shard_map/concatenate | solution.py:14
  17.7 4.1 %collective-permute-start.2 = (f32[1,256,258]{2,1,0:T(8,128)S(1)}, f32[1,256,258]{2,1,0:T(8,128)S(1)}, u32[]{:S(2)}, u32[]{:S(2)}) collective-permute-start(f32[1,256,258]{2,1,0:T(8,128)S(1)} %get-tuple-element.11), channel_id=1, source_target_pairs={{2,0},{4,2},{6,4},{0,6},{3,1},{5,3},{7,5},{1,7},{10,8},{12,10},{14... | collective-permute-start | bytes 792584 | tf_op jit(solution)/shard_map/ppermute | solution.py:18
  21.9 0.9 fusion.56
  22.8 0.6 collective-permute-start.12
  23.4 2.3 %collective-permute-start.13 = (f32[4,128,1]{2,1,0:T(8,128)}, f32[4,128,1]{2,1,0:T(8,128)}, u32[]{:S(2)}, u32[]{:S(2)}) collective-permute-start(f32[4,128,1]{2,1,0:T(8,128)} %get-tuple-element.20), channel_id=1, source_target_pairs={{8,0},{16,8},{24,16},{0,24},{9,1},{17,9},{25,17},{1,25},{10,2},{18... | collective-permute-start | bytes 6152 | tf_op jit(solution)/shard_map/ppermute | solution.py:18
  25.7 5.7 %collective-permute-done.2 = f32[1,256,258]{2,1,0:T(8,128)S(1)} collective-permute-done((f32[1,256,258]{2,1,0:T(8,128)S(1)}, f32[1,256,258]{2,1,0:T(8,128)S(1)}, u32[]{:S(2)}, u32[]{:S(2)}) %collective-permute-start.2) | collective-permute-done | bytes 264224 | tf_op jit(solution)/shard_map/ppermute | solution.py:18
  31.4 7.6 %collective-permute-done.3 = f32[1,256,258]{2,1,0:T(8,128)S(1)} collective-permute-done((f32[1,256,258]{2,1,0:T(8,128)S(1)}, f32[1,256,258]{2,1,0:T(8,128)S(1)}, u32[]{:S(2)}, u32[]{:S(2)}) %collective-permute-start.3) | collective-permute-done | bytes 264224 | tf_op jit(solution)/shard_map/ppermute | solution.py:16
  39.2 0.5 collective-permute-start.4
  39.7 1.6 %slice_add_fusion = f32[1,8,256,256]{3,2,1,0:T(8,128)} fusion(f32[2,8,256,256]{3,2,1,0:T(8,128)S(1)} %copy-done.3), kind=kLoop, calls=%fused_computation.61 | loop fusion | flops 524288 | bytes 6291456 | tf_op jit(solution)/shard_map/add | solution.py:67
  41.4 5.0 %fusion.2 = f32[8,256,256]{2,1,0:T(8,128)S(1)} fusion(f32[8,256,256]{2,1,0:T(8,128)S(1)} %copy-done, f32[8,256,1]{2,1,0:T(8,128)S(1)} %copy.34, f32[8,256,1]{2,1,0:T(8,128)S(1)} %copy-done.6, f32[10,1,258]{2,1,0:T(1,128)S(1)} %collective-permute-done.5, f32[1,256,258]{2,1,0:T(8,128)S(1)} %collective-permute-done.2, ...), kind=kLoop, calls=%fused_computation.5 | loop fusion | flops 17825792 | bytes 6856864 | tf_op jit(solution)/shard_map/add | solution.py:35
  46.4 1.6 %fusion.54 = (f32[8,256,1]{2,1,0:T(8,128)S(1)}, f32[8,256,1]{2,1,0:T(8,128)}) fusion(f32[8,256,256]{2,1,0:T(8,128)S(1)} %fusion.2), kind=kLoop, calls=%fused_computation.151 | loop fusion | bytes 32768 | tf_op jit(solution)/shard_map/slice | solution.py:12
  48.0 1.7 %copy.38 = f32[8,256,1]{1,0,2:T(8,128)S(1)} copy(f32[8,256,1]{2,1,0:T(8,128)} %get-tuple-element.13) | data formatting | bytes 16384 | tf_op jit(solution)/shard_map/slice | solution.py:13
  49.7 0.6 collective-permute-start.6
  50.3 0.3 copy.39
  50.6 2.4 %collective-permute-start.7 = (f32[8,256,1]{1,0,2:T(8,128)S(1)}, f32[8,256,1]{1,0,2:T(8,128)S(1)}, u32[]{:S(2)}, u32[]{:S(2)}) collective-permute-start(f32[8,256,1]{1,0,2:T(8,128)S(1)} %copy.39), channel_id=1, source_target_pairs={{8,0},{16,8},{24,16},{0,24},{9,1},{17,9},{25,17},{1,25},{10,2},{18... | collective-permute-start | bytes 24584 | tf_op jit(solution)/shard_map/ppermute | solution.py:18
  53.0 1.2 %fusion.41 = f32[2048,128]{1,0:T(8,128)S(1)} fusion(f32[2048,256]{1,0:T(8,128)S(1)} %bitcast.39, s32[256]{0:T(256)S(1)} %get-tuple-element.22, s32[256]{0:T(256)S(1)} %get-tuple-element.23, pred[256]{0:T(512)(128)(4,1)S(1)} %compare_and_fusion), kind=kOutput, calls=%fused_computation.119 | convolution fusion | flops 805371904 | bytes 3148032 | tf_op jit(solution)/shard_map/dot_general | solution.py:48
  54.2 1.3 %reshape.34 = f32[4,2,128,256]{3,2,1,0:T(8,128)} reshape(f32[2048,128]{1,0:T(8,128)S(1)} %fusion.41) | data formatting | bytes 2097152 | tf_op jit(solution)/shard_map/reshape | solution.py:54
  55.5 0.4 copy.40
  55.9 1.4 %copy.41 = f32[8,256,1]{2,1,0:T(8,128)} copy(f32[8,256,1]{1,0,2:T(8,128)S(1)} %collective-permute-done.7) | data formatting | bytes 16384 | tf_op jit(solution)/shard_map/ppermute | solution.py:18
  57.3 1.4 %pad_maximum_fusion.36 = (f32[1,256,258]{2,1,0:T(8,128)S(1)}, f32[1,256,258]{2,1,0:T(8,128)S(1)}) fusion(f32[8,256,1]{2,1,0:T(8,128)} %copy.41, f32[8,256,256]{2,1,0:T(8,128)S(1)} %copy-done.2, f32[8,256,1]{2,1,0:T(8,128)S(1)} %copy.40), kind=kLoop, calls=%fused_computation.72 | loop fusion | flops 264192 | bytes 2641920 | tf_op jit(solution)/shard_map/concatenate | solution.py:14
  58.7 1.8 %collective-permute-start.8 = (f32[1,256,258]{2,1,0:T(8,128)S(1)}, f32[1,256,258]{2,1,0:T(8,128)S(1)}, u32[]{:S(2)}, u32[]{:S(2)}) collective-permute-start(f32[1,256,258]{2,1,0:T(8,128)S(1)} %get-tuple-element.9), channel_id=1, source_target_pairs={{2,0},{4,2},{6,4},{0,6},{3,1},{5,3},{7,5},{1,7},{10,8},{12,10},{14... | collective-permute-start | bytes 792584 | tf_op jit(solution)/shard_map/ppermute | solution.py:18
  60.7 0.9 fusion.23
  61.6 1.1 %pad_maximum_fusion.60 = (f32[1,128,130]{2,1,0:T(8,128)S(1)}, f32[1,128,130]{2,1,0:T(8,128)S(1)}) fusion(f32[4,128,1]{2,1,0:T(8,128)} %collective-permute-done.13, f32[4,128,128]{2,1,0:T(8,128)S(1)} %broadcast_multiply_fusion, f32[4,128,1]{2,1,0:T(8,128)} %collective-permute-done.12), kind=kLoop, calls=%fused_computation.114 | loop fusion | flops 66560 | bytes 399360 | tf_op jit(solution)/shard_map/concatenate | solution.py:14
  62.7 3.6 %collective-permute-start.14 = (f32[1,128,130]{2,1,0:T(8,128)S(1)}, f32[1,128,130]{2,1,0:T(8,128)S(1)}, u32[]{:S(2)}, u32[]{:S(2)}) collective-permute-start(f32[1,128,130]{2,1,0:T(8,128)S(1)} %get-tuple-element.19), channel_id=1, source_target_pairs={{2,0},{4,2},{6,4},{0,6},{3,1},{5,3},{7,5},{1,7},{10,8},{12,10},{14... | collective-permute-start | bytes 199688 | tf_op jit(solution)/shard_map/ppermute | solution.py:18
  66.3 12.5 %collective-permute-done.8 = f32[1,256,258]{2,1,0:T(8,128)S(1)} collective-permute-done((f32[1,256,258]{2,1,0:T(8,128)S(1)}, f32[1,256,258]{2,1,0:T(8,128)S(1)}, u32[]{:S(2)}, u32[]{:S(2)}) %collective-permute-start.8) | collective-permute-done | bytes 264224 | tf_op jit(solution)/shard_map/ppermute | solution.py:18
  78.8 0.5 collective-permute-done.9
  79.6 0.5 collective-permute-start.10
  80.1 1.6 %collective-permute-done.14 = f32[1,128,130]{2,1,0:T(8,128)S(1)} collective-permute-done((f32[1,128,130]{2,1,0:T(8,128)S(1)}, f32[1,128,130]{2,1,0:T(8,128)S(1)}, u32[]{:S(2)}, u32[]{:S(2)}) %collective-permute-start.14) | collective-permute-done | bytes 66592 | tf_op jit(solution)/shard_map/ppermute | solution.py:18
  81.7 1.8 %collective-permute-done.15 = f32[1,128,130]{2,1,0:T(8,128)S(1)} collective-permute-done((f32[1,128,130]{2,1,0:T(8,128)S(1)}, f32[1,128,130]{2,1,0:T(8,128)S(1)}, u32[]{:S(2)}, u32[]{:S(2)}) %collective-permute-start.15) | collective-permute-done | bytes 66592 | tf_op jit(solution)/shard_map/ppermute | solution.py:16
  83.5 1.5 %pad_maximum_fusion.77 = (f32[6,1,130]{2,1,0:T(1,128)S(1)}, f32[6,1,130]{2,1,0:T(1,128)}) fusion(f32[1,128,130]{2,1,0:T(8,128)S(1)} %collective-permute-done.14, f32[1,128,130]{2,1,0:T(8,128)S(1)} %collective-permute-done.15, f32[4,128,1]{2,1,0:T(8,128)} %collective-permute-done.13, f32[4,128,128]{2,1,0:T(8,128)S(1)} %broadcast_multiply_fusion, ...), kind=kLoop, calls=%fused_computation.145 | loop fusion | flops 6240 | bytes 405600 | tf_op jit(solution)/shard_map/slice | solution.py:12
  85.0 0.5 collective-permute-start.16
  85.5 5.0 %fusion.5 = f32[8,256,256]{2,1,0:T(8,128)S(1)} fusion(f32[8,256,256]{2,1,0:T(8,128)S(1)} %copy-done.2, f32[8,256,1]{2,1,0:T(8,128)S(1)} %copy.40, f32[8,256,1]{2,1,0:T(8,128)S(1)} %copy-done.5, f32[10,1,258]{2,1,0:T(1,128)S(1)} %collective-permute-done.11, f32[1,256,258]{2,1,0:T(8,128)S(1)} %collective-permute-done.8, ...), kind=kLoop, calls=%fused_computation.8 | loop fusion | flops 17825792 | bytes 6856864 | tf_op jit(solution)/shard_map/add | solution.py:35
  90.6 1.3 %copy-done.8 = f32[8,256,256]{2,1,0:T(8,128)} copy-done((f32[8,256,256]{2,1,0:T(8,128)}, f32[8,256,256]{2,1,0:T(8,128)S(1)}, u32[]{:S(2)}) %copy-start.8) | copy-done | bytes 2097176
  91.9 1.2 %fusion.43 = f32[2048,128]{1,0:T(8,128)S(1)} fusion(f32[2048,256]{1,0:T(8,128)S(1)} %bitcast.40, s32[256]{0:T(256)S(1)} %get-tuple-element.22, s32[256]{0:T(256)S(1)} %get-tuple-element.23, pred[256]{0:T(512)(128)(4,1)S(1)} %copy-done.15), kind=kOutput, calls=%fused_computation.121 | convolution fusion | flops 805371904 | bytes 3148032 | tf_op jit(solution)/shard_map/dot_general | solution.py:48
  93.1 0.3 reshape.31
  93.5 0.6 copy-done.10
  94.3 2.8 %fusion.30 = f32[4,128,128]{2,1,0:T(8,128)} fusion(f32[4,128,128]{2,1,0:T(8,128)S(1)} %broadcast_multiply_fusion, f32[4,128,256]{2,1,0:T(8,128)S(1)} %copy-done.12, f32[4,128,1]{2,1,0:T(8,128)} %collective-permute-done.12, f32[4,128,1]{2,1,0:T(8,128)} %collective-permute-done.13, f32[6,1,130]{2,1,0:T(1,128)} %collective-permute-done.17, ...), kind=kLoop, calls=%fused_computation.82 | loop fusion | flops 2555904 | bytes 2240608 | tf_op jit(solution)/shard_map/sub | solution.py:71
  (54 shorter events, 1.1 us)
Async XLA Ops:
  3.5 6.0 %copy-start = (f32[8,256,256]{2,1,0:T(8,128)S(1)}, f32[8,256,256]{2,1,0:T(8,128)}, u32[]{:S(2)}) copy-start(f32[8,256,256]{2,1,0:T(8,128)} %param.2) | copy-start | bytes 6291460
  5.2 9.5 %collective-permute-start = (f32[8,256,1]{1,0,2:T(8,128)S(1)}, f32[8,256,1]{1,0,2:T(8,128)S(1)}, u32[]{:S(2)}, u32[]{:S(2)}) collective-permute-start(f32[8,256,1]{1,0,2:T(8,128)S(1)} %copy.49), channel_id=1, source_target_pairs={{0,8},{8,16},{16,24},{24,0},{1,9},{9,17},{17,25},{25,1},{2,10},{10... | collective-permute-start | bytes 24584 | tf_op jit(solution)/shard_map/ppermute | solution.py:16
  8.5 6.5 %collective-permute-start.1 = (f32[8,256,1]{1,0,2:T(8,128)S(1)}, f32[8,256,1]{1,0,2:T(8,128)S(1)}, u32[]{:S(2)}, u32[]{:S(2)}) collective-permute-start(f32[8,256,1]{1,0,2:T(8,128)S(1)} %copy.50), channel_id=1, source_target_pairs={{8,0},{16,8},{24,16},{0,24},{9,1},{17,9},{25,17},{1,25},{10,2},{18... | collective-permute-start | bytes 24584 | tf_op jit(solution)/shard_map/ppermute | solution.py:18
  9.5 43.5 %copy-start.14 = (pred[256]{0:T(512)(128)(4,1)}, pred[256]{0:T(512)(128)(4,1)S(1)}, u32[]{:S(2)}) copy-start(pred[256]{0:T(512)(128)(4,1)S(1)} %compare_and_fusion) | copy-start | bytes 772
  16.4 5.5 %copy-start.9 = (f32[4,128,256]{2,1,0:T(8,128)S(1)}, f32[4,128,256]{2,1,0:T(8,128)}, u32[]{:S(2)}) copy-start(f32[4,128,256]{2,1,0:T(8,128)} %fusion.24) | copy-start | bytes 1572868
  17.7 21.3 %copy-start.6 = (f32[8,256,1]{2,1,0:T(8,128)S(1)}, f32[8,256,1]{2,1,0:T(8,128)}, u32[]{:S(2)}) copy-start(f32[8,256,1]{2,1,0:T(8,128)} %copy.35) | copy-start | bytes 24580
  17.7 13.6 %collective-permute-start.2 = (f32[1,256,258]{2,1,0:T(8,128)S(1)}, f32[1,256,258]{2,1,0:T(8,128)S(1)}, u32[]{:S(2)}, u32[]{:S(2)}) collective-permute-start(f32[1,256,258]{2,1,0:T(8,128)S(1)} %get-tuple-element.11), channel_id=1, source_target_pairs={{2,0},{4,2},{6,4},{0,6},{3,1},{5,3},{7,5},{1,7},{10,8},{12,10},{14... | collective-permute-start | bytes 792584 | tf_op jit(solution)/shard_map/ppermute | solution.py:18
  21.9 17.1 %collective-permute-start.3 = (f32[1,256,258]{2,1,0:T(8,128)S(1)}, f32[1,256,258]{2,1,0:T(8,128)S(1)}, u32[]{:S(2)}, u32[]{:S(2)}) collective-permute-start(f32[1,256,258]{2,1,0:T(8,128)S(1)} %get-tuple-element.10), channel_id=1, source_target_pairs={{0,2},{2,4},{4,6},{6,0},{1,3},{3,5},{5,7},{7,1},{8,10},{10,12},{12... | collective-permute-start | bytes 792584 | tf_op jit(solution)/shard_map/ppermute | solution.py:16
  22.8 38.8 %collective-permute-start.12 = (f32[4,128,1]{2,1,0:T(8,128)}, f32[4,128,1]{2,1,0:T(8,128)}, u32[]{:S(2)}, u32[]{:S(2)}) collective-permute-start(f32[4,128,1]{2,1,0:T(8,128)} %get-tuple-element.21), channel_id=1, source_target_pairs={{0,8},{8,16},{16,24},{24,0},{1,9},{9,17},{17,25},{25,1},{2,10},{10... | collective-permute-start | bytes 6152 | tf_op jit(solution)/shard_map/ppermute | solution.py:16
  23.4 16.4 %copy-start.3 = (f32[2,8,256,256]{3,2,1,0:T(8,128)S(1)}, f32[2,8,256,256]{3,2,1,0:T(8,128)}, u32[]{:S(2)}) copy-start(f32[2,8,256,256]{3,2,1,0:T(8,128)} %param.3) | copy-start | bytes 12582916
  23.4 38.2 %collective-permute-start.13 = (f32[4,128,1]{2,1,0:T(8,128)}, f32[4,128,1]{2,1,0:T(8,128)}, u32[]{:S(2)}, u32[]{:S(2)}) collective-permute-start(f32[4,128,1]{2,1,0:T(8,128)} %get-tuple-element.20), channel_id=1, source_target_pairs={{8,0},{16,8},{24,16},{0,24},{9,1},{17,9},{25,17},{1,25},{10,2},{18... | collective-permute-start | bytes 6152 | tf_op jit(solution)/shard_map/ppermute | solution.py:18
  39.2 2.2 %collective-permute-start.5 = (f32[10,1,258]{2,1,0:T(1,128)S(1)}, f32[10,1,258]{2,1,0:T(1,128)S(1)}, u32[]{:S(2)}, u32[]{:S(2)}) collective-permute-start(f32[10,1,258]{2,1,0:T(1,128)S(1)} %get-tuple-element.7), channel_id=1, source_target_pairs={{0,1},{1,0},{2,3},{3,2},{4,5},{5,4},{6,7},{7,6},{8,9},{9,8},{10,11... | collective-permute-start | bytes 30968 | tf_op jit(solution)/shard_map/ppermute | solution.py:16
  39.2 2.1 %collective-permute-start.4 = (f32[10,1,258]{2,1,0:T(1,128)S(1)}, f32[10,1,258]{2,1,0:T(1,128)S(1)}, u32[]{:S(2)}, u32[]{:S(2)}) collective-permute-start(f32[10,1,258]{2,1,0:T(1,128)S(1)} %get-tuple-element.6), channel_id=1, source_target_pairs={{1,0},{0,1},{3,2},{2,3},{5,4},{4,5},{7,6},{6,7},{9,8},{8,9},{11,10... | collective-permute-start | bytes 30968 | tf_op jit(solution)/shard_map/ppermute | solution.py:18
  46.4 1.7 %copy-start.1 = (f32[8,256,256]{2,1,0:T(8,128)}, f32[8,256,256]{2,1,0:T(8,128)S(1)}, u32[]{:S(2)}) copy-start(f32[8,256,256]{2,1,0:T(8,128)S(1)} %fusion.2) | copy-start | bytes 6291460
  48.0 5.0 %copy-start.7 = (f32[1,8,256,256]{3,2,1,0:T(8,128)S(1)}, f32[1,8,256,256]{3,2,1,0:T(8,128)}, u32[]{:S(2)}) copy-start(f32[1,8,256,256]{3,2,1,0:T(8,128)} %slice_add_fusion) | copy-start | bytes 6291460
  49.7 5.8 %collective-permute-start.6 = (f32[8,256,1]{1,0,2:T(8,128)S(1)}, f32[8,256,1]{1,0,2:T(8,128)S(1)}, u32[]{:S(2)}, u32[]{:S(2)}) collective-permute-start(f32[8,256,1]{1,0,2:T(8,128)S(1)} %copy.38), channel_id=1, source_target_pairs={{0,8},{8,16},{16,24},{24,0},{1,9},{9,17},{17,25},{25,1},{2,10},{10... | collective-permute-start | bytes 24584 | tf_op jit(solution)/shard_map/ppermute | solution.py:16
  50.6 5.2 %collective-permute-start.7 = (f32[8,256,1]{1,0,2:T(8,128)S(1)}, f32[8,256,1]{1,0,2:T(8,128)S(1)}, u32[]{:S(2)}, u32[]{:S(2)}) collective-permute-start(f32[8,256,1]{1,0,2:T(8,128)S(1)} %copy.39), channel_id=1, source_target_pairs={{8,0},{16,8},{24,16},{0,24},{9,1},{17,9},{25,17},{1,25},{10,2},{18... | collective-permute-start | bytes 24584 | tf_op jit(solution)/shard_map/ppermute | solution.py:18
  54.2 3.0 %copy-start.2 = (f32[8,256,256]{2,1,0:T(8,128)S(1)}, f32[8,256,256]{2,1,0:T(8,128)}, u32[]{:S(2)}) copy-start(f32[8,256,256]{2,1,0:T(8,128)} %copy-done.1) | copy-start | bytes 6291460
  57.2 3.5 %copy-start.11 = (f32[4,2,128,256]{3,2,1,0:T(8,128)S(1)}, f32[4,2,128,256]{3,2,1,0:T(8,128)}, u32[]{:S(2)}) copy-start(f32[4,2,128,256]{3,2,1,0:T(8,128)} %reshape.34) | copy-start | bytes 3145732
  58.6 20.7 %copy-start.5 = (f32[8,256,1]{2,1,0:T(8,128)S(1)}, f32[8,256,1]{2,1,0:T(8,128)}, u32[]{:S(2)}) copy-start(f32[8,256,1]{2,1,0:T(8,128)} %copy.41) | copy-start | bytes 24580
  58.7 20.2 %collective-permute-start.8 = (f32[1,256,258]{2,1,0:T(8,128)S(1)}, f32[1,256,258]{2,1,0:T(8,128)S(1)}, u32[]{:S(2)}, u32[]{:S(2)}) collective-permute-start(f32[1,256,258]{2,1,0:T(8,128)S(1)} %get-tuple-element.9), channel_id=1, source_target_pairs={{2,0},{4,2},{6,4},{0,6},{3,1},{5,3},{7,5},{1,7},{10,8},{12,10},{14... | collective-permute-start | bytes 792584 | tf_op jit(solution)/shard_map/ppermute | solution.py:18
  60.5 18.9 %collective-permute-start.9 = (f32[1,256,258]{2,1,0:T(8,128)S(1)}, f32[1,256,258]{2,1,0:T(8,128)S(1)}, u32[]{:S(2)}, u32[]{:S(2)}) collective-permute-start(f32[1,256,258]{2,1,0:T(8,128)S(1)} %get-tuple-element.8), channel_id=1, source_target_pairs={{0,2},{2,4},{4,6},{6,0},{1,3},{3,5},{5,7},{7,1},{8,10},{10,12},{12... | collective-permute-start | bytes 792584 | tf_op jit(solution)/shard_map/ppermute | solution.py:16
  62.7 19.0 %collective-permute-start.14 = (f32[1,128,130]{2,1,0:T(8,128)S(1)}, f32[1,128,130]{2,1,0:T(8,128)S(1)}, u32[]{:S(2)}, u32[]{:S(2)}) collective-permute-start(f32[1,128,130]{2,1,0:T(8,128)S(1)} %get-tuple-element.19), channel_id=1, source_target_pairs={{2,0},{4,2},{6,4},{0,6},{3,1},{5,3},{7,5},{1,7},{10,8},{12,10},{14... | collective-permute-start | bytes 199688 | tf_op jit(solution)/shard_map/ppermute | solution.py:18
  66.3 19.2 %copy-start.4 = (f32[2,8,256,256]{3,2,1,0:T(8,128)S(1)}, f32[2,8,256,256]{3,2,1,0:T(8,128)}, u32[]{:S(2)}) copy-start(f32[2,8,256,256]{3,2,1,0:T(8,128)} %param.3) | copy-start | bytes 12582916
  66.3 17.2 %collective-permute-start.15 = (f32[1,128,130]{2,1,0:T(8,128)S(1)}, f32[1,128,130]{2,1,0:T(8,128)S(1)}, u32[]{:S(2)}, u32[]{:S(2)}) collective-permute-start(f32[1,128,130]{2,1,0:T(8,128)S(1)} %get-tuple-element.18), channel_id=1, source_target_pairs={{0,2},{2,4},{4,6},{6,0},{1,3},{3,5},{5,7},{7,1},{8,10},{10,12},{12... | collective-permute-start | bytes 199688 | tf_op jit(solution)/shard_map/ppermute | solution.py:16
  79.5 6.0 %collective-permute-start.11 = (f32[10,1,258]{2,1,0:T(1,128)S(1)}, f32[10,1,258]{2,1,0:T(1,128)S(1)}, u32[]{:S(2)}, u32[]{:S(2)}) collective-permute-start(f32[10,1,258]{2,1,0:T(1,128)S(1)} %get-tuple-element.5), channel_id=1, source_target_pairs={{0,1},{1,0},{2,3},{3,2},{4,5},{5,4},{6,7},{7,6},{8,9},{9,8},{10,11... | collective-permute-start | bytes 30968 | tf_op jit(solution)/shard_map/ppermute | solution.py:16
  79.6 6.0 %collective-permute-start.10 = (f32[10,1,258]{2,1,0:T(1,128)S(1)}, f32[10,1,258]{2,1,0:T(1,128)S(1)}, u32[]{:S(2)}, u32[]{:S(2)}) collective-permute-start(f32[10,1,258]{2,1,0:T(1,128)S(1)} %get-tuple-element.4), channel_id=1, source_target_pairs={{1,0},{0,1},{3,2},{2,3},{5,4},{4,5},{7,6},{6,7},{9,8},{8,9},{11,10... | collective-permute-start | bytes 30968 | tf_op jit(solution)/shard_map/ppermute | solution.py:18
  83.5 2.0 %copy-start.13 = (f32[1,128,130]{2,1,0:T(8,128)}, f32[1,128,130]{2,1,0:T(8,128)S(1)}, u32[]{:S(2)}) copy-start(f32[1,128,130]{2,1,0:T(8,128)S(1)} %collective-permute-done.15) | copy-start | bytes 199684
  85.0 8.5 %collective-permute-start.17 = (f32[6,1,130]{2,1,0:T(1,128)}, f32[6,1,130]{2,1,0:T(1,128)}, u32[]{:S(2)}, u32[]{:S(2)}) collective-permute-start(f32[6,1,130]{2,1,0:T(1,128)} %get-tuple-element.17), channel_id=1, source_target_pairs={{0,1},{1,0},{2,3},{3,2},{4,5},{5,4},{6,7},{7,6},{8,9},{9,8},{10,11... | collective-permute-start | bytes 9368 | tf_op jit(solution)/shard_map/ppermute | solution.py:16
  85.0 6.9 %copy-start.15 = (pred[256]{0:T(512)(128)(4,1)S(1)}, pred[256]{0:T(512)(128)(4,1)}, u32[]{:S(2)}) copy-start(pred[256]{0:T(512)(128)(4,1)} %copy-done.14) | copy-start | bytes 772
  85.0 8.5 %collective-permute-start.16 = (f32[6,1,130]{2,1,0:T(1,128)S(1)}, f32[6,1,130]{2,1,0:T(1,128)}, u32[]{:S(2)}, u32[]{:S(2)}) collective-permute-start(f32[6,1,130]{2,1,0:T(1,128)S(1)} %get-tuple-element.16), channel_id=1, source_target_pairs={{1,0},{0,1},{3,2},{2,3},{5,4},{4,5},{7,6},{6,7},{9,8},{8,9},{11,10... | collective-permute-start | bytes 9368 | tf_op jit(solution)/shard_map/ppermute | solution.py:18
  90.6 1.3 %copy-start.8 = (f32[8,256,256]{2,1,0:T(8,128)}, f32[8,256,256]{2,1,0:T(8,128)S(1)}, u32[]{:S(2)}) copy-start(f32[8,256,256]{2,1,0:T(8,128)S(1)} %fusion.5) | copy-start | bytes 6291460
  93.1 1.0 %copy-start.10 = (f32[4,128,256]{2,1,0:T(8,128)S(1)}, f32[4,128,256]{2,1,0:T(8,128)}, u32[]{:S(2)}) copy-start(f32[4,128,256]{2,1,0:T(8,128)} %fusion.24) | copy-start | bytes 1572868
  93.1 1.2 %copy-start.12 = (f32[4,128,256]{2,1,0:T(8,128)S(1)}, f32[4,128,256]{2,1,0:T(8,128)}, u32[]{:S(2)}) copy-start(f32[4,128,256]{2,1,0:T(8,128)} %fusion.23) | copy-start | bytes 1572868
where the time goes:
time: 97.5 us; the launch traced here: 97.1 us
  waiting for transfers between devices  29.8 us (31%)
  other arithmetic  21.8 us (22%)
  starting transfers between devices  21.3 us (22%)
  local copies, waits for them, and re-layouts  19.4 us (20%)
  matrix products  3.79 us (4%)
    ppermute x9, waiting for transfers between devices, padded_2(): lax.ppermute(head, axis, [((i + 1) % count, i) for i in range(count)])  19.8 us
    ppermute x9, starting transfers between devices, padded_2(): lax.ppermute(head, axis, [((i + 1) % count, i) for i in range(count)])  16.7 us
    ppermute x9, waiting for transfers between devices, padded_2(): lax.ppermute(tail, axis, [(i, (i + 1) % count) for i in range(count)])  10 us
    add x2, other arithmetic, advance(): center + spread * (neighbours(padded) - 6.0 * center)  9.99 us
    slice x4, local copies, waits for them, and re-layouts, padded_2(): head = lax.slice_in_dim(cells, 0, width, axis=dim)  5.66 us
    ppermute x9, starting transfers between devices, padded_2(): lax.ppermute(tail, axis, [(i, (i + 1) % count) for i in range(count)])  4.62 us
    unnamed x34, local copies, waits for them, and re-layouts  4.21 us
    concatenate x3, other arithmetic, padded_2(): jnp.concatenate([lax.ppermute(tail, axis, [(i, (i + 1) % count) for i in...  3.85 us
  transfers between devices with their start and end apart: 18, of which 6 were waited for; matrix products, arithmetic and copies ran while one was open for 34% of the time, Pallas kernels for 0%

commit v1 on v0

v1 whole, which is shorter than its diff:
```python
import functools

import jax
import jax.numpy as jnp
from jax import lax
from jax.experimental import pallas as pl
from jax.experimental.pallas import tpu as pltpu
from jax.sharding import PartitionSpec as P

noise_amp = 0.3
lanes = 128
pad = 8
steps = 4


def remote(src, dst, send, recv, axis, where):
    return pltpu.make_async_remote_copy(
        src_ref=src,
        dst_ref=dst,
        send_sem=send,
        recv_sem=recv,
        device_id={axis: where},
        device_id_type=pl.DeviceIdType.MESH,
    )


def pack(buf, planes, rows, wide):
    lane = lax.broadcasted_iota(jnp.int32, (rows, lanes), 1)
    both = jnp.zeros((rows, lanes), jnp.float32)
    for i in range(planes):
        head = buf[1 + i, pad : pad + rows, 0:lanes]
        tail = buf[1 + i, pad : pad + rows, wide - lanes : wide]
        if i:
            head = pltpu.roll(head, i, 1)
        both = jnp.where(lane == i, head, both)
        both = jnp.where(lane == planes + i, pltpu.roll(tail, planes + i + 1, 1), both)
    groups = lanes // (2 * planes)
    deep = rows // groups
    folded = both[0:deep]
    for g in range(1, groups):
        folded = folded + pltpu.roll(both[g * deep : (g + 1) * deep], g * 2 * planes, 1)
    return folded


def unpack(folded, out, side, planes, rows):
    groups = lanes // (2 * planes)
    deep = rows // groups
    for g in range(groups):
        part = folded if g == 0 else pltpu.roll(folded, lanes - g * 2 * planes, 1)
        out[side, g * deep : (g + 1) * deep, :] = part


def beside(buf, beyond, i, r0, rows, planes, wide):
    y = buf[i, pl.ds(r0, rows + 2 * pad), :]
    tall = rows + 2 * pad
    c = y[pad : pad + rows]
    total = pltpu.roll(y, 1, 0)[pad : pad + rows] + pltpu.roll(y, tall - 1, 0)[pad : pad + rows]
    inner = pl.ds(r0 + pad, rows)
    total = total + buf[i - 1, inner, :] + buf[i + 1, inner, :]
    lane = lax.broadcasted_iota(jnp.int32, (rows, lanes), 1)
    left = pltpu.roll(beyond[0, pl.ds(r0, rows), :], 2 * lanes - planes - (i - 1), 1)
    right = pltpu.roll(beyond[1, pl.ds(r0, rows), :], lanes - 1 - (i - 1), 1)
    back = pltpu.roll(c, 1, 1)
    ahead = pltpu.roll(c, wide - 1, 1)
    first = jnp.where(lane == 0, left, back[:, 0:lanes])
    last = jnp.where(lane == lanes - 1, right, ahead[:, wide - lanes : wide])
    if wide > lanes:
        back = jnp.concatenate([first, back[:, lanes:]], axis=1)
        ahead = jnp.concatenate([ahead[:, : wide - lanes], last], axis=1)
    else:
        back, ahead = first, last
    return c, total + back + ahead


def advanced(c, around, spread, react):
    return c + spread * (around - 6.0 * c) + react * (c - c * c * c)


def halved(block, table, tmp):
    rows = block.shape[0]
    out = None
    rest = block
    for n in range(3):
        part = rest.astype(jnp.bfloat16)
        term = jnp.dot(part, table[...], preferred_element_type=jnp.float32)
        out = term if out is None else out + term
        if n < 2:
            rest = rest - part.astype(jnp.float32)
    tmp[...] = out
    return (tmp[pl.ds(0, rows // 2, stride=2), :] + tmp[pl.ds(1, rows // 2, stride=2), :]) * 0.125


def kernel(
    sizes, field, noise, next_out, cor_out,
    vbuf, mbuf, cbuf, n0, n1, obuf, kbuf, pkv, pkm, pkc, hv, hm, hc, uv, um, uc, table, tmp,
    zs, zr, ls, lr, gs, gr, loc,
):
    nx, ny, nz = field.shape
    cx, cy, cz = nx // 2, ny // 2, nz // 2
    rows = ny // steps
    crows = rows // 2

    def ends(axis):
        me = lax.axis_index(axis)
        n = sizes[axis]
        return lax.rem(me + 1, n), lax.rem(me + n - 1, n)

    nxt = {a: ends(a)[0] for a in ("gz", "lvl", "gy")}
    prv = {a: ends(a)[1] for a in ("gz", "lvl", "gy")}

    load_v = pltpu.make_async_copy(field, vbuf.at[1 : nx + 1, pad : pad + ny, :], loc.at[0])
    load_n0 = pltpu.make_async_copy(noise.at[0], n0, loc.at[1])
    load_n1 = pltpu.make_async_copy(noise.at[1], n1, loc.at[2])
    load_v.start()
    load_n0.start()
    load_n1.start()

    barrier = pltpu.get_barrier_semaphore()
    for axis in ("gz", "lvl", "gy"):
        for side in (nxt, prv):
            pl.semaphore_signal(
                barrier, inc=1, device_id={axis: side[axis]}, device_id_type=pl.DeviceIdType.MESH
            )
    source = lax.broadcasted_iota(jnp.int32, (nz, cz), 0) // 2
    target = lax.broadcasted_iota(jnp.int32, (nz, cz), 1)
    table[...] = jnp.where(source == target, 1.0, 0.0).astype(jnp.bfloat16)
    pl.semaphore_wait(barrier, 6)

    def planes_out(src_low, src_high, buf, count, slot, where):
        up = remote(src_high, buf.at[(0,) + where], zs.at[0, slot], zr.at[0, slot], "gz", nxt["gz"])
        down = remote(src_low, buf.at[(count + 1,) + where], zs.at[1, slot], zr.at[1, slot], "gz", prv["gz"])
        up.start()
        down.start()
        return up, down

    def slabs_out(src_low, src_high, buf, count, tall, slot):
        up = remote(src_high, buf.at[1 : count + 1, 0:pad, :], gs.at[0, slot], gr.at[0, slot], "gy", nxt["gy"])
        down = remote(
            src_low, buf.at[1 : count + 1, pad + tall : 2 * pad + tall, :],
            gs.at[1, slot], gr.at[1, slot], "gy", prv["gy"],
        )
        up.start()
        down.start()
        return up, down

    def columns_out(packed, held, slot):
        up = remote(packed, held.at[0], ls.at[0, slot], lr.at[0, slot], "lvl", nxt["lvl"])
        down = remote(packed, held.at[1], ls.at[1, slot], lr.at[1, slot], "lvl", prv["lvl"])
        up.start()
        down.start()
        return up, down

    vz = []
    for c in range(steps):
        at = pl.ds(c * rows, rows)
        vz.append(
            planes_out(
                field.at[0, at, :], field.at[nx - 1, at, :], vbuf, nx, c, (pl.ds(pad + c * rows, rows), slice(None))
            )
        )
    vg = slabs_out(field.at[:, 0:pad, :], field.at[:, ny - pad : ny, :], vbuf, nx, ny, 0)

    load_v.wait()
    pkv[...] = pack(vbuf, nx, ny, nz)
    vl = columns_out(pkv, hv, 0)

    @pl.loop(0, cx * steps)
    def _(t):
        k, c = t // steps, t % steps
        at = pl.ds(pl.multiple_of(c * rows + pad, pad), rows)
        block = vbuf[2 * k + 1, at, :] + vbuf[2 * k + 2, at, :]
        cbuf[k + 1, pl.ds(pl.multiple_of(c * crows + pad, pad), crows), :] = halved(block, table, tmp)

    cin = (pl.ds(pad, cy), slice(None))
    cz_ = planes_out(cbuf.at[(1,) + cin], cbuf.at[(cx,) + cin], cbuf, cx, 2 * steps, cin)
    cg = slabs_out(cbuf.at[1 : cx + 1, pad : 2 * pad, :], cbuf.at[1 : cx + 1, cy : cy + pad, :], cbuf, cx, cy, 2)
    pkc[...] = pack(cbuf, cx, cy, cz)
    cl = columns_out(pkc, hc, 2)

    load_n0.wait()
    for copy in vg + vl:
        copy.wait_recv()
    for side in range(2):
        unpack(hv[side], uv, side, nx, ny)

    def middle(i, r0):
        c, around = beside(vbuf, uv, i, r0, rows, nx, nz)
        made = advanced(c, around, 0.15, 0.1) + noise_amp * n0[i - 1, pl.ds(r0, rows), :]
        mbuf[i, pl.ds(r0 + pad, rows), :] = made

    @pl.loop(0, (nx - 2) * steps)
    def _(t):
        middle(2 + t // steps, pl.multiple_of((t % steps) * rows, rows))

    mz = []
    for c in range(steps):
        for copy, i in zip(vz[c], (1, nx)):
            copy.wait_recv()
            middle(i, c * rows)
        where = (pl.ds(pad + c * rows, rows), slice(None))
        mz.append(planes_out(mbuf.at[(1,) + where], mbuf.at[(nx,) + where], mbuf, nx, steps + c, where))

    pkm[...] = pack(mbuf, nx, ny, nz)
    ml = columns_out(pkm, hm, 1)
    mg = slabs_out(mbuf.at[1 : nx + 1, pad : 2 * pad, :], mbuf.at[1 : nx + 1, ny : ny + pad, :], mbuf, nx, ny, 1)
    load_n1.wait()
    for copy in cz_ + cl + cg:
        copy.wait_recv()
    for side in range(2):
        unpack(hc[side], uc, side, cx, cy)
    for copy in ml + mg:
        copy.wait_recv()
    for side in range(2):
        unpack(hm[side], um, side, nx, ny)

    def finish(i, r0):
        c, around = beside(mbuf, um, i, r0, rows, nx, nz)
        made = advanced(c, around, 0.15, 0.1) + noise_amp * n1[i - 1, pl.ds(r0, rows), :]
        obuf[i - 1, pl.ds(r0, rows), :] = made

    def correct(k, r0, half):
        at = pl.ds(r0, rows)
        block = None
        for i in (2 * k, 2 * k + 1):
            term = obuf[i, at, :] - noise_amp * (n0[i, at, :] + n1[i, at, :])
            block = term if block is None else block + term
        c, around = beside(cbuf, uc, k + 1, half, crows, cx, cz)
        kbuf[k, pl.ds(half, crows), :] = halved(block, table, tmp) - advanced(c, around, 0.075, 0.2)

    @pl.loop(0, (nx - 2) * steps)
    def _(t):
        finish(2 + t // steps, pl.multiple_of((t % steps) * rows, rows))

    outs = [pltpu.make_async_copy(obuf.at[1 : nx - 1], next_out.at[1 : nx - 1], loc.at[3])]
    outs[0].start()

    @pl.loop(0, (cx - 2) * steps)
    def _(t):
        c = t % steps
        correct(1 + t // steps, pl.multiple_of(c * rows, rows), pl.multiple_of(c * crows, crows))

    outs.append(pltpu.make_async_copy(kbuf.at[1 : cx - 1], cor_out.at[1 : cx - 1], loc.at[4]))
    outs[1].start()

    for c in range(steps):
        for side, i, k in ((0, 1, 0), (1, nx, cx - 1)):
            mz[c][side].wait_recv()
            finish(i, c * rows)
            at = pl.ds(c * rows, rows)
            copy = pltpu.make_async_copy(obuf.at[i - 1, at, :], next_out.at[i - 1, at, :], loc.at[5 + 4 * c + 2 * side])
            copy.start()
            outs.append(copy)
            correct(k, c * rows, c * crows)
            at = pl.ds(c * crows, crows)
            copy = pltpu.make_async_copy(kbuf.at[k, at, :], cor_out.at[k, at, :], loc.at[6 + 4 * c + 2 * side])
            copy.start()
            outs.append(copy)

    for group in vz + mz + [vg, vl, cz_, cg, cl, ml, mg]:
        for copy in group:
            copy.wait_send()
    for copy in outs:
        copy.wait()


def on_device(sizes, fine_field, noise_pair):
    nx, ny, nz = fine_field.shape
    cx, cy, cz = nx // 2, ny // 2, nz // 2
    fold = ny // (lanes // (2 * nx))
    cfold = cy // (lanes // (2 * cx))
    f32 = jnp.float32
    whole = pl.BlockSpec(memory_space=pl.ANY)
    dma = pltpu.SemaphoreType.DMA
    return pl.pallas_call(
        functools.partial(kernel, sizes),
        out_shape=(jax.ShapeDtypeStruct((nx, ny, nz), f32), jax.ShapeDtypeStruct((cx, cy, cz), f32)),
        in_specs=[whole, whole],
        out_specs=(whole, whole),
        scratch_shapes=[
            pltpu.VMEM((nx + 2, ny + 2 * pad, nz), f32),
            pltpu.VMEM((nx + 2, ny + 2 * pad, nz), f32),
            pltpu.VMEM((cx + 2, cy + 2 * pad, cz), f32),
            pltpu.VMEM((nx, ny, nz), f32),
            pltpu.VMEM((nx, ny, nz), f32),
            pltpu.VMEM((nx, ny, nz), f32),
            pltpu.VMEM((cx, cy, cz), f32),
            pltpu.VMEM((fold, lanes), f32),
            pltpu.VMEM((fold, lanes), f32),
            pltpu.VMEM((cfold, lanes), f32),
            pltpu.VMEM((2, fold, lanes), f32),
            pltpu.VMEM((2, fold, lanes), f32),
            pltpu.VMEM((2, cfold, lanes), f32),
            pltpu.VMEM((2, ny, lanes), f32),
            pltpu.VMEM((2, ny, lanes), f32),
            pltpu.VMEM((2, cy, lanes), f32),
            pltpu.VMEM((nz, cz), jnp.bfloat16),
            pltpu.VMEM((ny // steps, cz), f32),
            dma((2, 2 * steps + 1)),
            dma((2, 2 * steps + 1)),
            dma((2, 3)),
            dma((2, 3)),
            dma((2, 3)),
            dma((2, 3)),
            dma((5 + 4 * steps,)),
        ],
        compiler_params=pltpu.CompilerParams(collective_id=0, has_side_effects=True),
    )(fine_field, noise_pair)


def solution(mesh):
    in_specs = (P("gz", "gy", "lvl"), P(None, "gz", "gy", "lvl"))
    out_specs = (P("gz", "gy", "lvl"), P("gz", "gy", "lvl"))
    sizes = dict(mesh.shape)
    return jax.shard_map(
        functools.partial(on_device, sizes), mesh=mesh, in_specs=in_specs, out_specs=out_specs, check_vma=False
    )
```

time: 97.5 us -> 39.3 us (0.40)
  Pallas kernels: 0 us -> 34.7 us
  waiting for transfers between devices: 29.8 us -> 0 us
  other arithmetic: 21.8 us -> 0 us
  starting transfers between devices: 21.3 us -> 0 us
  local copies, waits for them, and re-layouts: 19.4 us -> 3.79 us
  matrix products: 3.79 us -> 0 us
    pallas_call x0 -> x1, Pallas kernels: none -> 34.7 us  [on_device(): pl.pallas_call(functools.partial(kernel, sizes), out_shape=(jax.ShapeDtyp...]
    ppermute x18 -> x0, waiting for transfers between devices: 29.8 us -> none  [the longest x9 19.8 us: padded_2(): lax.ppermute(head, axis, [((i + 1) % count, i) for i in range(count)])]
    ppermute x18 -> x0, starting transfers between devices: 21.3 us -> none  [the longest x9 16.7 us: padded_2(): lax.ppermute(head, axis, [((i + 1) % count, i) for i in range(count)])]
    add x6 -> x0, other arithmetic: 13.4 us -> none  [the longest x2 9.99 us: advance(): center + spread * (neighbours(padded) - 6.0 * center)]
    slice x5 -> x0, local copies, waits for them, and re-layouts: 7.35 us -> none  [the longest x4 5.66 us: padded_2(): head = lax.slice_in_dim(cells, 0, width, axis=dim)]
    concatenate x3 -> x0, other arithmetic: 3.85 us -> none  [padded_2(): jnp.concatenate([lax.ppermute(tail, axis, [(i, (i + 1) % count) for i in...]
    dot_general x3 -> x0, matrix products: 3.79 us -> none  [coarsen(): jnp.dot(values.reshape(first * second, third), table, precision=lax.Preci...]
    ppermute x4 -> x0, local copies, waits for them, and re-layouts: 3.44 us -> none  [the longest x2 2.71 us: padded_2(): lax.ppermute(head, axis, [((i + 1) % count, i) for i in range(count)])]
  transfers between devices with their start and end apart: 18 -> 0, of which waited for: 6 -> 0; matrix products, arithmetic and copies ran while one was open for 34% -> 0% of each run, Pallas kernels for 0% -> 0%
where the time goes in v1:
time: 39.3 us; the launch traced here: 39.1 us
  Pallas kernels  34.7 us (88%)
  local copies, waits for them, and re-layouts  3.79 us (10%)
  between operations  0.65 us (2%)
    pallas_call x1, Pallas kernels, on_device(): pl.pallas_call(functools.partial(kernel, sizes), out_shape=(jax.ShapeDtyp...  34.7 us
    unnamed x4, local copies, waits for them, and re-layouts  3.79 us

profile of v1, /device:TPU:0, one launch (start us, length us, event | category | flops | bytes accessed | tf_op | source)
XLA Modules:
  0.0 39.1 jit_solution(8786620818038878537)
XLA Ops:
  0.6 34.7 %shard_map.41 = (f32[8,256,256]{2,1,0:T(8,128)}, f32[4,128,128]{2,1,0:T(8,128)}) custom-call(f32[8,256,256]{2,1,0:T(8,128)} %field.1, f32[2,8,256,256]{3,2,1,0:T(8,128)} %noise.1), custom_call_target="tpu_custom_call" | custom-call | tf_op jit(solution)/shard_map/pallas_call | solution.py:274
  35.3 0.0 copy-start
  35.3 3.1 %copy.6 = f32[8,256,256]{2,1,0:T(8,128)} copy(f32[8,256,256]{2,1,0:T(8,128)} %get-tuple-element.4) | data formatting | bytes 4194304
  38.4 0.0 copy-done
  38.4 0.7 %copy.7 = f32[4,128,128]{2,1,0:T(8,128)} copy(f32[4,128,128]{2,1,0:T(8,128)S(1)} %copy-done) | data formatting | bytes 524288
Async XLA Ops:
  35.3 3.1 %copy-start = (f32[4,128,128]{2,1,0:T(8,128)S(1)}, f32[4,128,128]{2,1,0:T(8,128)}, u32[]{:S(2)}) copy-start(f32[4,128,128]{2,1,0:T(8,128)} %get-tuple-element.5) | copy-start | bytes 786436

commit v2 on v1

--- a/solution.py
+++ b/solution.py
@@ -10,7 +10,7 @@
 noise_amp = 0.3
 lanes = 128
 pad = 8
-steps = 4
+steps = 1
 
 
 def remote(src, dst, send, recv, axis, where):
@@ -91,8 +91,8 @@
 
 
 def kernel(
-    sizes, field, noise, next_out, cor_out,
-    vbuf, mbuf, cbuf, n0, n1, obuf, kbuf, pkv, pkm, pkc, hv, hm, hc, uv, um, uc, table, tmp,
+    sizes, field, noise, obuf, kbuf,
+    vbuf, mbuf, cbuf, n0, n1, pkv, pkm, pkc, hv, hm, hc, uv, um, uc, table, tmp,
     zs, zr, ls, lr, gs, gr, loc,
 ):
     nx, ny, nz = field.shape
@@ -231,35 +231,29 @@
     def _(t):
         finish(2 + t // steps, pl.multiple_of((t % steps) * rows, rows))
 
-    outs = [pltpu.make_async_copy(obuf.at[1 : nx - 1], next_out.at[1 : nx - 1], loc.at[3])]
-    outs[0].start()
-
     @pl.loop(0, (cx - 2) * steps)
     def _(t):
         c = t % steps
         correct(1 + t // steps, pl.multiple_of(c * rows, rows), pl.multiple_of(c * crows, crows))
 
-    outs.append(pltpu.make_async_copy(kbuf.at[1 : cx - 1], cor_out.at[1 : cx - 1], loc.at[4]))
-    outs[1].start()
-
     for c in range(steps):
         for side, i, k in ((0, 1, 0), (1, nx, cx - 1)):
             mz[c][side].wait_recv()
             finish(i, c * rows)
-            at = pl.ds(c * rows, rows)
-            copy = pltpu.make_async_copy(obuf.at[i - 1, at, :], next_out.at[i - 1, at, :], loc.at[5 + 4 * c + 2 * side])
-            copy.start()
-            outs.append(copy)
             correct(k, c * rows, c * crows)
-            at = pl.ds(c * crows, crows)
-            copy = pltpu.make_async_copy(kbuf.at[k, at, :], cor_out.at[k, at, :], loc.at[6 + 4 * c + 2 * side])
-            copy.start()
-            outs.append(copy)
 
     for group in vz + mz + [vg, vl, cz_, cg, cl, ml, mg]:
         for copy in group:
             copy.wait_send()
-    for copy in outs:
+
+
+def put_out(fine, coarse, fine_out, coarse_out, sems):
+    copies = [pltpu.make_async_copy(coarse, coarse_out, sems.at[0])]
+    for i in range(fine.shape[0]):
+        copies.append(pltpu.make_async_copy(fine.at[i], fine_out.at[i], sems.at[1 + i]))
+    for copy in copies:
+        copy.start()
+    for copy in copies:
         copy.wait()
 
 
@@ -269,21 +263,20 @@
     fold = ny // (lanes // (2 * nx))
     cfold = cy // (lanes // (2 * cx))
     f32 = jnp.float32
-    whole = pl.BlockSpec(memory_space=pl.ANY)
+    whole = pl.BlockSpec(memory_space=pltpu.HBM)
+    held = pl.BlockSpec(memory_space=pltpu.VMEM)
     dma = pltpu.SemaphoreType.DMA
-    return pl.pallas_call(
+    made = pl.pallas_call(
         functools.partial(kernel, sizes),
         out_shape=(jax.ShapeDtypeStruct((nx, ny, nz), f32), jax.ShapeDtypeStruct((cx, cy, cz), f32)),
         in_specs=[whole, whole],
-        out_specs=(whole, whole),
+        out_specs=(held, held),
         scratch_shapes=[
             pltpu.VMEM((nx + 2, ny + 2 * pad, nz), f32),
             pltpu.VMEM((nx + 2, ny + 2 * pad, nz), f32),
             pltpu.VMEM((cx + 2, cy + 2 * pad, cz), f32),
             pltpu.VMEM((nx, ny, nz), f32),
             pltpu.VMEM((nx, ny, nz), f32),
-            pltpu.VMEM((nx, ny, nz), f32),
-            pltpu.VMEM((cx, cy, cz), f32),
             pltpu.VMEM((fold, lanes), f32),
             pltpu.VMEM((fold, lanes), f32),
             pltpu.VMEM((cfold, lanes), f32),
@@ -301,10 +294,18 @@
             dma((2, 3)),
             dma((2, 3)),
             dma((2, 3)),
-            dma((5 + 4 * steps,)),
+            dma((3,)),
         ],
-        compiler_params=pltpu.CompilerParams(collective_id=0, has_side_effects=True),
+        compiler_params=pltpu.CompilerParams(collective_id=0, has_side_effects=True, vmem_limit_bytes=50 * 2**20),
     )(fine_field, noise_pair)
+    return pl.pallas_call(
+        put_out,
+        out_shape=(jax.ShapeDtypeStruct((nx, ny, nz), f32), jax.ShapeDtypeStruct((cx, cy, cz), f32)),
+        in_specs=[held, held],
+        out_specs=(whole, whole),
+        scratch_shapes=[dma((nx + 1,))],
+        compiler_params=pltpu.CompilerParams(vmem_limit_bytes=8 * 2**20),
+    )(*made)
 
 
 def solution(mesh):

time: 39.3 us -> 34.7 us (0.88)
  local copies, waits for them, and re-layouts: 3.79 us -> 0 us
  Pallas kernels: 34.7 us -> 33.9 us
    unnamed x4 -> x0, local copies, waits for them, and re-layouts: 3.79 us -> none
    pallas_call x1, Pallas kernels: 34.7 us -> 32.4 us  [on_device(): pl.pallas_call(functools.partial(kernel, sizes), out_shape=(jax.ShapeDtyp...]
    pallas_call x0 -> x1, Pallas kernels: none -> 1.47 us  [on_device(): pl.pallas_call(put_out, out_shape=(jax.ShapeDtypeStruct((nx, ny, nz), f32...]
where the time goes in v2:
time: 34.7 us; the launch traced here: 34.5 us
  Pallas kernels  33.9 us (98%)
  between operations  0.64 us (2%)
    pallas_call x1, Pallas kernels, on_device(): pl.pallas_call(functools.partial(kernel, sizes), out_shape=(jax.ShapeDtyp...  32.4 us
    pallas_call x1, Pallas kernels, on_device(): pl.pallas_call(put_out, out_shape=(jax.ShapeDtypeStruct((nx, ny, nz), f32...  1.47 us

profile of v2, /device:TPU:0, one launch (start us, length us, event | category | flops | bytes accessed | tf_op | source)
XLA Modules:
  0.0 34.5 jit_solution(3704539246418772363)
XLA Ops:
  0.6 32.4 %shard_map.41 = (f32[8,256,256]{2,1,0:T(8,128)S(1)}, f32[4,128,128]{2,1,0:T(8,128)S(1)}) custom-call(f32[8,256,256]{2,1,0:T(8,128)} %field.1, f32[2,8,256,256]{3,2,1,0:T(8,128)} %noise.1), custom_call_target="tpu_custom_call" | custom-call | tf_op jit(solution)/shard_map/pallas_call | solution.py:269
  33.0 1.5 %shard_map.42 = (f32[8,256,256]{2,1,0:T(8,128)}, f32[4,128,128]{2,1,0:T(8,128)}) custom-call(f32[8,256,256]{2,1,0:T(8,128)S(1)} %get-tuple-element.4.fine, f32[4,128,128]{2,1,0:T(8,128)S(1)} %get-tuple-element.5.coarse), custom_call_target="tpu_custom_call" | custom-call | tf_op jit(solution)/shard_map/pallas_call | solution.py:301

commit v3 on v2

--- a/solution.py
+++ b/solution.py
@@ -50,13 +50,16 @@
         out[side, g * deep : (g + 1) * deep, :] = part
 
 
-def beside(buf, beyond, i, r0, rows, planes, wide):
+def beside(buf, beyond, i, r0, rows, planes, wide, lower=True, upper=True):
     y = buf[i, pl.ds(r0, rows + 2 * pad), :]
     tall = rows + 2 * pad
     c = y[pad : pad + rows]
     total = pltpu.roll(y, 1, 0)[pad : pad + rows] + pltpu.roll(y, tall - 1, 0)[pad : pad + rows]
     inner = pl.ds(r0 + pad, rows)
-    total = total + buf[i - 1, inner, :] + buf[i + 1, inner, :]
+    if lower:
+        total = total + buf[i - 1, inner, :]
+    if upper:
+        total = total + buf[i + 1, inner, :]
     lane = lax.broadcasted_iota(jnp.int32, (rows, lanes), 1)
     left = pltpu.roll(beyond[0, pl.ds(r0, rows), :], 2 * lanes - planes - (i - 1), 1)
     right = pltpu.roll(beyond[1, pl.ds(r0, rows), :], lanes - 1 - (i - 1), 1)
@@ -86,7 +89,7 @@
         out = term if out is None else out + term
         if n < 2:
             rest = rest - part.astype(jnp.float32)
-    tmp[...] = out
+    tmp[0:rows, :] = out
     return (tmp[pl.ds(0, rows // 2, stride=2), :] + tmp[pl.ds(1, rows // 2, stride=2), :]) * 0.125
 
 
@@ -126,12 +129,18 @@
     table[...] = jnp.where(source == target, 1.0, 0.0).astype(jnp.bfloat16)
     pl.semaphore_wait(barrier, 6)
 
-    def planes_out(src_low, src_high, buf, count, slot, where):
-        up = remote(src_high, buf.at[(0,) + where], zs.at[0, slot], zr.at[0, slot], "gz", nxt["gz"])
-        down = remote(src_low, buf.at[(count + 1,) + where], zs.at[1, slot], zr.at[1, slot], "gz", prv["gz"])
+    def planes_up(src, buf, count, slot, where):
+        up = remote(src, buf.at[(0,) + where], zs.at[0, slot], zr.at[0, slot], "gz", nxt["gz"])
         up.start()
+        return up
+
+    def planes_down(src, buf, count, slot, where):
+        down = remote(src, buf.at[(count + 1,) + where], zs.at[1, slot], zr.at[1, slot], "gz", prv["gz"])
         down.start()
-        return up, down
+        return down
+
+    def planes_out(src_low, src_high, *rest):
+        return planes_up(src_high, *rest), planes_down(src_low, *rest)
 
     def slabs_out(src_low, src_high, buf, count, tall, slot):
         up = remote(src_high, buf.at[1 : count + 1, 0:pad, :], gs.at[0, slot], gr.at[0, slot], "gy", nxt["gy"])
@@ -164,12 +173,10 @@
     pkv[...] = pack(vbuf, nx, ny, nz)
     vl = columns_out(pkv, hv, 0)
 
-    @pl.loop(0, cx * steps)
-    def _(t):
-        k, c = t // steps, t % steps
-        at = pl.ds(pl.multiple_of(c * rows + pad, pad), rows)
-        block = vbuf[2 * k + 1, at, :] + vbuf[2 * k + 2, at, :]
-        cbuf[k + 1, pl.ds(pl.multiple_of(c * crows + pad, pad), crows), :] = halved(block, table, tmp)
+    @pl.loop(0, cx)
+    def _(k):
+        block = vbuf[2 * k + 1, pad : pad + ny, :] + vbuf[2 * k + 2, pad : pad + ny, :]
+        cbuf[k + 1, pad : pad + cy, :] = halved(block, table, tmp)
 
     cin = (pl.ds(pad, cy), slice(None))
     cz_ = planes_out(cbuf.at[(1,) + cin], cbuf.at[(cx,) + cin], cbuf, cx, 2 * steps, cin)
@@ -183,22 +190,24 @@
     for side in range(2):
         unpack(hv[side], uv, side, nx, ny)
 
-    def middle(i, r0):
+    def middle(i, r0, rows):
         c, around = beside(vbuf, uv, i, r0, rows, nx, nz)
         made = advanced(c, around, 0.15, 0.1) + noise_amp * n0[i - 1, pl.ds(r0, rows), :]
         mbuf[i, pl.ds(r0 + pad, rows), :] = made
 
-    @pl.loop(0, (nx - 2) * steps)
+    @pl.loop(0, nx - 2)
     def _(t):
-        middle(2 + t // steps, pl.multiple_of((t % steps) * rows, rows))
+        middle(2 + t, 0, ny)
 
     mz = []
-    for c in range(steps):
-        for copy, i in zip(vz[c], (1, nx)):
+    for s in range(steps):
+        where = (pl.ds(pad + s * rows, rows), slice(None))
+        pair = []
+        for copy, i, gone in zip(vz[s][::-1], (nx, 1), (planes_up, planes_down)):
             copy.wait_recv()
-            middle(i, c * rows)
-        where = (pl.ds(pad + c * rows, rows), slice(None))
-        mz.append(planes_out(mbuf.at[(1,) + where], mbuf.at[(nx,) + where], mbuf, nx, steps + c, where))
+            middle(i, s * rows, rows)
+            pair.append(gone(mbuf.at[(i,) + where], mbuf, nx, steps + s, where))
+        mz.append((pair[0], pair[1]))
 
     pkm[...] = pack(mbuf, nx, ny, nz)
     ml = columns_out(pkm, hm, 1)
@@ -213,34 +222,36 @@
     for side in range(2):
         unpack(hm[side], um, side, nx, ny)
 
-    def finish(i, r0):
-        c, around = beside(mbuf, um, i, r0, rows, nx, nz)
-        made = advanced(c, around, 0.15, 0.1) + noise_amp * n1[i - 1, pl.ds(r0, rows), :]
-        obuf[i - 1, pl.ds(r0, rows), :] = made
-
-    def correct(k, r0, half):
-        at = pl.ds(r0, rows)
+    def finish(i, lower=True, upper=True):
+        c, around = beside(mbuf, um, i, 0, ny, nx, nz, lower, upper)
+        obuf[i - 1] = advanced(c, around, 0.15, 0.1) + noise_amp * n1[i - 1]
+
+    def correct(k):
         block = None
         for i in (2 * k, 2 * k + 1):
-            term = obuf[i, at, :] - noise_amp * (n0[i, at, :] + n1[i, at, :])
+            term = obuf[i] - noise_amp * (n0[i] + n1[i])
             block = term if block is None else block + term
-        c, around = beside(cbuf, uc, k + 1, half, crows, cx, cz)
-        kbuf[k, pl.ds(half, crows), :] = halved(block, table, tmp) - advanced(c, around, 0.075, 0.2)
-
-    @pl.loop(0, (nx - 2) * steps)
-    def _(t):
-        finish(2 + t // steps, pl.multiple_of((t % steps) * rows, rows))
-
-    @pl.loop(0, (cx - 2) * steps)
-    def _(t):
-        c = t % steps
-        correct(1 + t // steps, pl.multiple_of(c * rows, rows), pl.multiple_of(c * crows, crows))
-
-    for c in range(steps):
-        for side, i, k in ((0, 1, 0), (1, nx, cx - 1)):
-            mz[c][side].wait_recv()
-            finish(i, c * rows)
-            correct(k, c * rows, c * crows)
+        c, around = beside(cbuf, uc, k + 1, 0, cy, cx, cz)
+        kbuf[k] = halved(block, table, tmp) - advanced(c, around, 0.075, 0.2)
+
+    @pl.loop(2, nx)
+    def _(i):
+        finish(i)
+
+    finish(1, lower=False)
+    finish(nx, upper=False)
+
+    @pl.loop(0, cx)
+    def _(k):
+        correct(k)
+
+    for s in range(steps):
+        for side, i, k, beyond in ((0, 0, 0, 0), (1, nx - 1, cx - 1, nx + 1)):
+            mz[s][side].wait_recv()
+            at, low = pl.ds(s * rows, rows), pl.ds(s * crows, crows)
+            more = 0.15 * mbuf[beyond, pl.ds(pad + s * rows, rows), :]
+            obuf[i, at, :] = obuf[i, at, :] + more
+            kbuf[k, low, :] = kbuf[k, low, :] + halved(more, table, tmp)
 
     for group in vz + mz + [vg, vl, cz_, cg, cl, ml, mg]:
         for copy in group:
@@ -287,7 +298,7 @@
             pltpu.VMEM((2, ny, lanes), f32),
             pltpu.VMEM((2, cy, lanes), f32),
             pltpu.VMEM((nz, cz), jnp.bfloat16),
-            pltpu.VMEM((ny // steps, cz), f32),
+            pltpu.VMEM((ny, cz), f32),
             dma((2, 2 * steps + 1)),
             dma((2, 2 * steps + 1)),
             dma((2, 3)),

time: 34.7 us -> 34.6 us (level)
  no operation moved by 1% of the time
where the time goes in v3:
time: 34.6 us; the launch traced here: 34.4 us
  Pallas kernels  33.8 us (98%)
  between operations  0.64 us (2%)
    pallas_call x1, Pallas kernels, on_device(): pl.pallas_call(functools.partial(kernel, sizes), out_shape=(jax.ShapeDtyp...  32.3 us
    pallas_call x1, Pallas kernels, on_device(): pl.pallas_call(put_out, out_shape=(jax.ShapeDtypeStruct((nx, ny, nz), f32...  1.47 us

profile of v3, /device:TPU:0, one launch (start us, length us, event | category | flops | bytes accessed | tf_op | source)
XLA Modules:
  0.0 34.4 jit_solution(13819530281155292707)
XLA Ops:
  0.6 32.3 %shard_map.41 = (f32[8,256,256]{2,1,0:T(8,128)S(1)}, f32[4,128,128]{2,1,0:T(8,128)S(1)}) custom-call(f32[8,256,256]{2,1,0:T(8,128)} %field.1, f32[2,8,256,256]{3,2,1,0:T(8,128)} %noise.1), custom_call_target="tpu_custom_call" | custom-call | tf_op jit(solution)/shard_map/pallas_call | solution.py:280
  32.9 1.5 %shard_map.42 = (f32[8,256,256]{2,1,0:T(8,128)}, f32[4,128,128]{2,1,0:T(8,128)}) custom-call(f32[8,256,256]{2,1,0:T(8,128)S(1)} %get-tuple-element.4.fine, f32[4,128,128]{2,1,0:T(8,128)S(1)} %get-tuple-element.5.coarse), custom_call_target="tpu_custom_call" | custom-call | tf_op jit(solution)/shard_map/pallas_call | solution.py:312

commit v4 on v3

--- a/solution.py
+++ b/solution.py
@@ -111,6 +111,12 @@
     nxt = {a: ends(a)[0] for a in ("gz", "lvl", "gy")}
     prv = {a: ends(a)[1] for a in ("gz", "lvl", "gy")}
 
+    barrier = pltpu.get_barrier_semaphore()
+    for axis in ("gz", "lvl", "gy"):
+        for side in (nxt, prv):
+            pl.semaphore_signal(
+                barrier, inc=1, device_id={axis: side[axis]}, device_id_type=pl.DeviceIdType.MESH
+            )
     load_v = pltpu.make_async_copy(field, vbuf.at[1 : nx + 1, pad : pad + ny, :], loc.at[0])
     load_n0 = pltpu.make_async_copy(noise.at[0], n0, loc.at[1])
     load_n1 = pltpu.make_async_copy(noise.at[1], n1, loc.at[2])
@@ -118,12 +124,6 @@
     load_n0.start()
     load_n1.start()
 
-    barrier = pltpu.get_barrier_semaphore()
-    for axis in ("gz", "lvl", "gy"):
-        for side in (nxt, prv):
-            pl.semaphore_signal(
-                barrier, inc=1, device_id={axis: side[axis]}, device_id_type=pl.DeviceIdType.MESH
-            )
     source = lax.broadcasted_iota(jnp.int32, (nz, cz), 0) // 2
     target = lax.broadcasted_iota(jnp.int32, (nz, cz), 1)
     table[...] = jnp.where(source == target, 1.0, 0.0).astype(jnp.bfloat16)
@@ -298,7 +298,7 @@
             pltpu.VMEM((2, ny, lanes), f32),
             pltpu.VMEM((2, cy, lanes), f32),
             pltpu.VMEM((nz, cz), jnp.bfloat16),
-            pltpu.VMEM((ny, cz), f32),
+            pltpu.VMEM((ny + pad, cz), f32),
             dma((2, 2 * steps + 1)),
             dma((2, 2 * steps + 1)),
             dma((2, 3)),

time: 34.6 us -> 34.5 us (level)
  no operation moved by 1% of the time
where the time goes in v4:
time: 34.5 us; the launch traced here: 34.4 us
  Pallas kernels  33.8 us (98%)
  between operations  0.64 us (2%)
    pallas_call x1, Pallas kernels, on_device(): pl.pallas_call(functools.partial(kernel, sizes), out_shape=(jax.ShapeDtyp...  32.3 us
    pallas_call x1, Pallas kernels, on_device(): pl.pallas_call(put_out, out_shape=(jax.ShapeDtypeStruct((nx, ny, nz), f32...  1.47 us

profile of v4, /device:TPU:0, one launch (start us, length us, event | category | flops | bytes accessed | tf_op | source)
XLA Modules:
  0.0 34.4 jit_solution(15218535790944957652)
XLA Ops:
  0.6 32.3 %shard_map.41 = (f32[8,256,256]{2,1,0:T(8,128)S(1)}, f32[4,128,128]{2,1,0:T(8,128)S(1)}) custom-call(f32[8,256,256]{2,1,0:T(8,128)} %field.1, f32[2,8,256,256]{3,2,1,0:T(8,128)} %noise.1), custom_call_target="tpu_custom_call" | custom-call | tf_op jit(solution)/shard_map/pallas_call | solution.py:280
  32.9 1.5 %shard_map.42 = (f32[8,256,256]{2,1,0:T(8,128)}, f32[4,128,128]{2,1,0:T(8,128)}) custom-call(f32[8,256,256]{2,1,0:T(8,128)S(1)} %get-tuple-element.4.fine, f32[4,128,128]{2,1,0:T(8,128)S(1)} %get-tuple-element.5.coarse), custom_call_target="tpu_custom_call" | custom-call | tf_op jit(solution)/shard_map/pallas_call | solution.py:312
